TPU v7x, 32 devices: a whole 2x2x4 slice. The times are simulated.
32 devices in a mesh: section: 4 (over y, x), row: 2 (over core), col: 4 (over z).
Axes of the slice: x: 2, y: 2, z: 4, core: 2. Of those that a mesh axis runs over, the one named last changes fastest.
Arguments:
- cotangent: float32 [4, 128, 4096], P('section', None, ('row', 'col')), may hold values from -6 to 6
- incoming: float32 [4, 128, 4096], P('section', None, ('row', 'col')), may hold values from -6 to 6
- upd_u: float32 [4, 8, 128, 4096], P('section', None, None, ('row', 'col')), may hold values from -4 to 4
- upd_v: float32 [4, 8, 128, 4096], P('section', None, None, ('row', 'col')), may hold values from -0.0078125 to 0.0078125
- saved_x: bfloat16 [4, 4, 128, 4096], P('section', None, None, ('row', 'col')), may hold values from -6 to 6
- saved_h: bfloat16 [4, 4, 2, 128, 14336], P('section', None, None, None, 'col'), may hold values from -6 to 6
- norm_gain: float32 [4, 4096], P('section', ('row', 'col')), may hold values from 0.25 to 1.75
- w_gate: bfloat16 [4, 4096, 14336], P('section', 'row', 'col'), may hold values from -0.09375 to 0.09375
- w_up: bfloat16 [4, 4096, 14336], P('section', 'row', 'col'), may hold values from -0.09375 to 0.09375
- w_down: bfloat16 [4, 14336, 4096], P('section', 'col', 'row'), may hold values from -0.046875 to 0.046875
Outputs:
- new_cotangent: float32 [4, 128, 4096], P('section', None, ('row', 'col'))
- residual_out: float32 [4, 128, 4096], P('section', None, ('row', 'col'))
All inputs are finite; a program needn't handle non-finite values.
Results may differ from a plain program's by a relative error of at most 0.014.
Values may be sent and summed in bfloat16 or wider, within the bound.
No kernel may reach another device: no remote copies, remote signals or barrier semaphores. Data moves between devices by JAX's collectives and lax.ppermute only.
A program may use at most 128 MiB of HBM per device.

v0:
```python
import jax
import jax.numpy as jnp
from jax import lax
from jax.sharding import PartitionSpec as P

D = 4096
eps = 1e-05


def shifted(x, axis, by):
    devices = lax.axis_size(axis)
    return lax.ppermute(x, axis, [(i, (i + by) % devices) for i in range(devices)])


def rotate(carry):
    return shifted(carry, "section", -1)


def shards(cotangent, incoming, upd_u, upd_v, saved_x, saved_h, norm_gain, w_gate, w_up, w_down):
    sections = lax.axis_size("section")
    section_idx = lax.axis_index("section")
    inputs_all = saved_x[0].astype(jnp.float32)
    hidden_all = saved_h[0]
    gain = norm_gain[0]
    wg = w_gate[0]
    wu = w_up[0]
    wd = w_down[0]

    def layer_step(step, carry):
        carry = rotate(carry)
        micro = (section_idx + step + 1) % sections
        xf = lax.dynamic_index_in_dim(inputs_all, micro, 0, keepdims=False)
        hpair = lax.dynamic_index_in_dim(hidden_all, micro, 0, keepdims=False)
        sumsq = lax.psum(jnp.sum(xf * xf, axis=1), ("row", "col"))
        gy = carry.astype(jnp.bfloat16)
        wide = lax.all_gather(gy, "col", axis=1, tiled=True)
        ga_part = lax.dot_general(
            wide, wd, (((1,), (1,)), ((), ())), preferred_element_type=jnp.float32
        )
        ga = lax.psum_scatter(ga_part, "row", scatter_dimension=1, tiled=True)
        width = ga.shape[1]
        offset = lax.axis_index("row") * width
        hg = lax.dynamic_slice_in_dim(hpair[0], offset, width, 1).astype(jnp.float32)
        hu = lax.dynamic_slice_in_dim(hpair[1], offset, width, 1).astype(jnp.float32)
        sig = jax.nn.sigmoid(hg)
        part_gate = (ga * hu * sig * (1.0 + hg * (1.0 - sig))).astype(jnp.bfloat16)
        part_up = (ga * hg * sig).astype(jnp.bfloat16)
        grad_gate, grad_up = (
            lax.all_gather(part_gate, "row", axis=1, tiled=True),
            lax.all_gather(part_up, "row", axis=1, tiled=True),
        )
        first = lax.dot_general(
            wg, grad_gate, (((1,), (1,)), ((), ())), preferred_element_type=jnp.float32
        )
        second = lax.dot_general(
            wu, grad_up, (((1,), (1,)), ((), ())), preferred_element_type=jnp.float32
        )
        normgrad = lax.psum_scatter(first + second, "col", scatter_dimension=0, tiled=True).T
        rstd = lax.rsqrt(sumsq / D + eps)[:, None]
        scaled = gain * normgrad
        inner = lax.psum(jnp.sum(scaled * xf, axis=1), ("row", "col"))[:, None] / D
        updated = carry + rstd * scaled - xf * (rstd * rstd * rstd) * inner
        active = jnp.logical_and(step >= micro, step - micro < sections)
        return jnp.where(active, updated, carry)

    pulled = lax.fori_loop(0, 2 * sections - 1, layer_step, cotangent[0])
    pulled = rotate(pulled)
    resid = pulled + incoming[0] - cotangent[0]
    local_dots = jnp.einsum("urd,rd->u", upd_v[0], resid, precision=lax.Precision.HIGHEST)
    dots = lax.psum(local_dots, ("row", "col"))
    update = jnp.einsum("u,urd->rd", dots, upd_u[0], precision=lax.Precision.HIGHEST)
    fresh = cotangent[0] + resid - update
    return (fresh[None], resid[None])


def solution(mesh):
    placed = (
        P("section", None, ("row", "col")),
        P("section", None, ("row", "col")),
        P("section", None, None, ("row", "col")),
        P("section", None, None, ("row", "col")),
        P("section", None, None, ("row", "col")),
        P("section", None, None, None, "col"),
        P("section", ("row", "col")),
        P("section", "row", "col"),
        P("section", "row", "col"),
        P("section", "col", "row"),
    )
    return jax.shard_map(
        shards,
        mesh=mesh,
        in_specs=placed,
        out_specs=(P("section", None, ("row", "col")), P("section", None, ("row", "col"))),
        check_vma=False,
    )
```

profile of v0, /device:TPU:0, one launch (start us, length us, event | category | flops | bytes accessed | tf_op | source)
XLA Modules:
  0.0 880.5 jit_solution(12553855589407518897)
XLA Ops:
  10.2 832.8 %while.15 = (s32[]{:T(128)}, f32[128,512]{1,0:T(8,128)}, s32[]{:T(128)}, f32[4,128,512]{2,1,0:T(8,128)S(1)}, f32[1,512]{1,0:T(1,128)}, /*index=5*/bf16[3584,2048...) while((s32[]{:T(128)}, f32[128,512]{1,0:T(8,128)}, ...), condition=%wide.region_7.8_spmd, body=%wide.region_0.7_spmd.sunk | while | flops 5641699840 | bytes 72765032 | solution.py:66
  20.1 15.1 %all_gather.33 = bf16[128,2048]{1,0:T(8,128)(2,1)S(1)} all-gather(bf16[128,512]{1,0:T(8,128)(2,1)S(1)} %convert_element_type.72), channel_id=1, replica_groups=mesh['section'=4,'row'=2,'col'=4] {'col'}, dimensions={1}, use_global_device_ids=true | all-gather | bytes 655360 | tf_op jit(solution)/shard_map/while/body/eval_jaxpr/all_gather | solution.py:36
  46.7 12.0 %reduce-scatter.3.cloned.1.call-done = f32[128,1792]{1,0:T(8,128)} async-done(((f32[128,3584]{1,0:T(8,128)}), f32[128,1792]{1,0:T(8,128)}) %reduce-scatter.3.cloned.1.call-update) | async-done | bytes 917520 | tf_op jit(solution)/shard_map/while/body/eval_jaxpr/reduce_scatter | solution.py:40
  86.4 28.7 %reduce-scatter.5.cloned.1.call-done = f32[512,128]{0,1:T(8,128)} async-done(((f32[2048,128]{0,1:T(8,128)}), f32[512,128]{0,1:T(8,128)}) %reduce-scatter.5.cloned.1.call-update) | async-done | bytes 262160 | tf_op jit(solution)/shard_map/while/body/eval_jaxpr/reduce_scatter | solution.py:58
  116.2 13.7 %all-reduce.2 = (f32[128]{0:T(128)S(1)}, f32[128]{0:T(128)S(1)}) all-reduce(f32[128]{0:T(128)S(1)} %get-tuple-element.317, f32[128]{0:T(128)S(1)} %get-tuple-element.318), channel_id=1, replica_groups=mesh['section'=4,'row'=2,'col'=4] {'row','col'}, use_global_device_ids=true, to_apply=%region_6.6 | all-reduce | flops 256 | bytes 2048 | tf_op jit(solution)/shard_map/while/body/eval_jaxpr/psum | solution.py:61
  141.1 16.1 %all_gather.33 = bf16[128,2048]{1,0:T(8,128)(2,1)S(1)} all-gather(bf16[128,512]{1,0:T(8,128)(2,1)S(1)} %convert_element_type.72), channel_id=1, replica_groups=mesh['section'=4,'row'=2,'col'=4] {'col'}, dimensions={1}, use_global_device_ids=true | all-gather | bytes 655360 | tf_op jit(solution)/shard_map/while/body/eval_jaxpr/all_gather | solution.py:36
  205.0 28.7 %reduce-scatter.5.cloned.1.call-done = f32[512,128]{0,1:T(8,128)} async-done(((f32[2048,128]{0,1:T(8,128)}), f32[512,128]{0,1:T(8,128)}) %reduce-scatter.5.cloned.1.call-update) | async-done | bytes 262160 | tf_op jit(solution)/shard_map/while/body/eval_jaxpr/reduce_scatter | solution.py:58
  234.8 13.7 %all-reduce.2 = (f32[128]{0:T(128)S(1)}, f32[128]{0:T(128)S(1)}) all-reduce(f32[128]{0:T(128)S(1)} %get-tuple-element.317, f32[128]{0:T(128)S(1)} %get-tuple-element.318), channel_id=1, replica_groups=mesh['section'=4,'row'=2,'col'=4] {'row','col'}, use_global_device_ids=true, to_apply=%region_6.6 | all-reduce | flops 256 | bytes 2048 | tf_op jit(solution)/shard_map/while/body/eval_jaxpr/psum | solution.py:61
  259.7 16.2 %all_gather.33 = bf16[128,2048]{1,0:T(8,128)(2,1)S(1)} all-gather(bf16[128,512]{1,0:T(8,128)(2,1)S(1)} %convert_element_type.72), channel_id=1, replica_groups=mesh['section'=4,'row'=2,'col'=4] {'col'}, dimensions={1}, use_global_device_ids=true | all-gather | bytes 655360 | tf_op jit(solution)/shard_map/while/body/eval_jaxpr/all_gather | solution.py:36
  323.5 28.7 %reduce-scatter.5.cloned.1.call-done = f32[512,128]{0,1:T(8,128)} async-done(((f32[2048,128]{0,1:T(8,128)}), f32[512,128]{0,1:T(8,128)}) %reduce-scatter.5.cloned.1.call-update) | async-done | bytes 262160 | tf_op jit(solution)/shard_map/while/body/eval_jaxpr/reduce_scatter | solution.py:58
  353.3 13.7 %all-reduce.2 = (f32[128]{0:T(128)S(1)}, f32[128]{0:T(128)S(1)}) all-reduce(f32[128]{0:T(128)S(1)} %get-tuple-element.317, f32[128]{0:T(128)S(1)} %get-tuple-element.318), channel_id=1, replica_groups=mesh['section'=4,'row'=2,'col'=4] {'row','col'}, use_global_device_ids=true, to_apply=%region_6.6 | all-reduce | flops 256 | bytes 2048 | tf_op jit(solution)/shard_map/while/body/eval_jaxpr/psum | solution.py:61
  378.2 16.2 %all_gather.33 = bf16[128,2048]{1,0:T(8,128)(2,1)S(1)} all-gather(bf16[128,512]{1,0:T(8,128)(2,1)S(1)} %convert_element_type.72), channel_id=1, replica_groups=mesh['section'=4,'row'=2,'col'=4] {'col'}, dimensions={1}, use_global_device_ids=true | all-gather | bytes 655360 | tf_op jit(solution)/shard_map/while/body/eval_jaxpr/all_gather | solution.py:36
  442.0 28.7 %reduce-scatter.5.cloned.1.call-done = f32[512,128]{0,1:T(8,128)} async-done(((f32[2048,128]{0,1:T(8,128)}), f32[512,128]{0,1:T(8,128)}) %reduce-scatter.5.cloned.1.call-update) | async-done | bytes 262160 | tf_op jit(solution)/shard_map/while/body/eval_jaxpr/reduce_scatter | solution.py:58
  471.8 13.7 %all-reduce.2 = (f32[128]{0:T(128)S(1)}, f32[128]{0:T(128)S(1)}) all-reduce(f32[128]{0:T(128)S(1)} %get-tuple-element.317, f32[128]{0:T(128)S(1)} %get-tuple-element.318), channel_id=1, replica_groups=mesh['section'=4,'row'=2,'col'=4] {'row','col'}, use_global_device_ids=true, to_apply=%region_6.6 | all-reduce | flops 256 | bytes 2048 | tf_op jit(solution)/shard_map/while/body/eval_jaxpr/psum | solution.py:61
  496.7 16.2 %all_gather.33 = bf16[128,2048]{1,0:T(8,128)(2,1)S(1)} all-gather(bf16[128,512]{1,0:T(8,128)(2,1)S(1)} %convert_element_type.72), channel_id=1, replica_groups=mesh['section'=4,'row'=2,'col'=4] {'col'}, dimensions={1}, use_global_device_ids=true | all-gather | bytes 655360 | tf_op jit(solution)/shard_map/while/body/eval_jaxpr/all_gather | solution.py:36
  560.6 28.7 %reduce-scatter.5.cloned.1.call-done = f32[512,128]{0,1:T(8,128)} async-done(((f32[2048,128]{0,1:T(8,128)}), f32[512,128]{0,1:T(8,128)}) %reduce-scatter.5.cloned.1.call-update) | async-done | bytes 262160 | tf_op jit(solution)/shard_map/while/body/eval_jaxpr/reduce_scatter | solution.py:58
  590.4 13.7 %all-reduce.2 = (f32[128]{0:T(128)S(1)}, f32[128]{0:T(128)S(1)}) all-reduce(f32[128]{0:T(128)S(1)} %get-tuple-element.317, f32[128]{0:T(128)S(1)} %get-tuple-element.318), channel_id=1, replica_groups=mesh['section'=4,'row'=2,'col'=4] {'row','col'}, use_global_device_ids=true, to_apply=%region_6.6 | all-reduce | flops 256 | bytes 2048 | tf_op jit(solution)/shard_map/while/body/eval_jaxpr/psum | solution.py:61
  615.3 16.2 %all_gather.33 = bf16[128,2048]{1,0:T(8,128)(2,1)S(1)} all-gather(bf16[128,512]{1,0:T(8,128)(2,1)S(1)} %convert_element_type.72), channel_id=1, replica_groups=mesh['section'=4,'row'=2,'col'=4] {'col'}, dimensions={1}, use_global_device_ids=true | all-gather | bytes 655360 | tf_op jit(solution)/shard_map/while/body/eval_jaxpr/all_gather | solution.py:36
  679.1 28.7 %reduce-scatter.5.cloned.1.call-done = f32[512,128]{0,1:T(8,128)} async-done(((f32[2048,128]{0,1:T(8,128)}), f32[512,128]{0,1:T(8,128)}) %reduce-scatter.5.cloned.1.call-update) | async-done | bytes 262160 | tf_op jit(solution)/shard_map/while/body/eval_jaxpr/reduce_scatter | solution.py:58
  708.9 13.7 %all-reduce.2 = (f32[128]{0:T(128)S(1)}, f32[128]{0:T(128)S(1)}) all-reduce(f32[128]{0:T(128)S(1)} %get-tuple-element.317, f32[128]{0:T(128)S(1)} %get-tuple-element.318), channel_id=1, replica_groups=mesh['section'=4,'row'=2,'col'=4] {'row','col'}, use_global_device_ids=true, to_apply=%region_6.6 | all-reduce | flops 256 | bytes 2048 | tf_op jit(solution)/shard_map/while/body/eval_jaxpr/psum | solution.py:61
  733.8 16.2 %all_gather.33 = bf16[128,2048]{1,0:T(8,128)(2,1)S(1)} all-gather(bf16[128,512]{1,0:T(8,128)(2,1)S(1)} %convert_element_type.72), channel_id=1, replica_groups=mesh['section'=4,'row'=2,'col'=4] {'col'}, dimensions={1}, use_global_device_ids=true | all-gather | bytes 655360 | tf_op jit(solution)/shard_map/while/body/eval_jaxpr/all_gather | solution.py:36
  797.6 28.7 %reduce-scatter.5.cloned.1.call-done = f32[512,128]{0,1:T(8,128)} async-done(((f32[2048,128]{0,1:T(8,128)}), f32[512,128]{0,1:T(8,128)}) %reduce-scatter.5.cloned.1.call-update) | async-done | bytes 262160 | tf_op jit(solution)/shard_map/while/body/eval_jaxpr/reduce_scatter | solution.py:58
  827.4 13.7 %all-reduce.2 = (f32[128]{0:T(128)S(1)}, f32[128]{0:T(128)S(1)}) all-reduce(f32[128]{0:T(128)S(1)} %get-tuple-element.317, f32[128]{0:T(128)S(1)} %get-tuple-element.318), channel_id=1, replica_groups=mesh['section'=4,'row'=2,'col'=4] {'row','col'}, use_global_device_ids=true, to_apply=%region_6.6 | all-reduce | flops 256 | bytes 2048 | tf_op jit(solution)/shard_map/while/body/eval_jaxpr/psum | solution.py:61
  855.4 14.0 %psum.35 = f32[8]{0:T(128)S(1)} all-reduce(f32[8]{0:T(128)S(1)} %fusion.16), channel_id=1, replica_groups=mesh['section'=4,'row'=2,'col'=4] {'row','col'}, use_global_device_ids=true, to_apply=%region_8.9 | all-reduce | flops 8 | bytes 64 | tf_op jit(solution)/shard_map/psum | solution.py:70
  (144 shorter events, 431.0 us)
Async XLA Ops:
  7.2 862.2 %copy-start = (f32[1,8,128,512]{3,2,1,0:T(8,128)S(1)}, f32[1,8,128,512]{3,2,1,0:T(8,128)}, u32[]{:S(2)}) copy-start(f32[1,8,128,512]{3,2,1,0:T(8,128)} %param.14) | copy-start | bytes 6291460
  10.2 48.5 %reduce-scatter.3.cloned.1.call-start = ((), (), s32[]{:S(2)}) async-start(), calls=%async_computation.2 | async-start | bytes 2752512 | tf_op jit(solution)/shard_map/while/body/eval_jaxpr/reduce_scatter | solution.py:40
  10.2 9.9 %collective-permute-start = (f32[128,512]{1,0:T(8,128)}, f32[128,512]{1,0:T(8,128)S(1)}, u32[]{:S(2)}, u32[]{:S(2)}) collective-permute-start(f32[128,512]{1,0:T(8,128)} %get-tuple-element.343), channel_id=1, source_target_pairs={{0,24},{8,0},{16,8},{24,16},{1,25},{9,1},{17,9},{25,17},{2,26},{10... | collective-permute-start | bytes 786440 | tf_op jit(solution)/shard_map/while/body/eval_jaxpr/ppermute | solution.py:12
  46.6 68.5 %reduce-scatter.5.cloned.1.call-start = ((), (), s32[]{:S(2)}) async-start(), calls=%async_computation.3 | async-start | bytes 1310720 | tf_op jit(solution)/shard_map/while/body/eval_jaxpr/reduce_scatter | solution.py:58
  131.7 45.6 %reduce-scatter.3.cloned.1.call-start = ((), (), s32[]{:S(2)}) async-start(), calls=%async_computation.2 | async-start | bytes 2752512 | tf_op jit(solution)/shard_map/while/body/eval_jaxpr/reduce_scatter | solution.py:40
  131.7 9.4 %collective-permute-start = (f32[128,512]{1,0:T(8,128)}, f32[128,512]{1,0:T(8,128)S(1)}, u32[]{:S(2)}, u32[]{:S(2)}) collective-permute-start(f32[128,512]{1,0:T(8,128)} %get-tuple-element.343), channel_id=1, source_target_pairs={{0,24},{8,0},{16,8},{24,16},{1,25},{9,1},{17,9},{25,17},{2,26},{10... | collective-permute-start | bytes 786440 | tf_op jit(solution)/shard_map/while/body/eval_jaxpr/ppermute | solution.py:12
  168.6 65.1 %reduce-scatter.5.cloned.1.call-start = ((), (), s32[]{:S(2)}) async-start(), calls=%async_computation.3 | async-start | bytes 1310720 | tf_op jit(solution)/shard_map/while/body/eval_jaxpr/reduce_scatter | solution.py:58
  194.0 39.7 %copy-start.2 = (f32[1,512]{1,0:T(1,128)S(1)}, f32[1,512]{1,0:T(1,128)}, u32[]{:S(2)}) copy-start(f32[1,512]{1,0:T(1,128)} %get-tuple-element.364) | copy-start | bytes 6148 | tf_op jit(solution)/shard_map/while
  250.3 45.6 %reduce-scatter.3.cloned.1.call-start = ((), (), s32[]{:S(2)}) async-start(), calls=%async_computation.2 | async-start | bytes 2752512 | tf_op jit(solution)/shard_map/while/body/eval_jaxpr/reduce_scatter | solution.py:40
  250.3 9.4 %collective-permute-start = (f32[128,512]{1,0:T(8,128)}, f32[128,512]{1,0:T(8,128)S(1)}, u32[]{:S(2)}, u32[]{:S(2)}) collective-permute-start(f32[128,512]{1,0:T(8,128)} %get-tuple-element.343), channel_id=1, source_target_pairs={{0,24},{8,0},{16,8},{24,16},{1,25},{9,1},{17,9},{25,17},{2,26},{10... | collective-permute-start | bytes 786440 | tf_op jit(solution)/shard_map/while/body/eval_jaxpr/ppermute | solution.py:12
  287.2 65.0 %reduce-scatter.5.cloned.1.call-start = ((), (), s32[]{:S(2)}) async-start(), calls=%async_computation.3 | async-start | bytes 1310720 | tf_op jit(solution)/shard_map/while/body/eval_jaxpr/reduce_scatter | solution.py:58
  368.8 45.5 %reduce-scatter.3.cloned.1.call-start = ((), (), s32[]{:S(2)}) async-start(), calls=%async_computation.2 | async-start | bytes 2752512 | tf_op jit(solution)/shard_map/while/body/eval_jaxpr/reduce_scatter | solution.py:40
  368.8 9.4 %collective-permute-start = (f32[128,512]{1,0:T(8,128)}, f32[128,512]{1,0:T(8,128)S(1)}, u32[]{:S(2)}, u32[]{:S(2)}) collective-permute-start(f32[128,512]{1,0:T(8,128)} %get-tuple-element.343), channel_id=1, source_target_pairs={{0,24},{8,0},{16,8},{24,16},{1,25},{9,1},{17,9},{25,17},{2,26},{10... | collective-permute-start | bytes 786440 | tf_op jit(solution)/shard_map/while/body/eval_jaxpr/ppermute | solution.py:12
  405.8 65.0 %reduce-scatter.5.cloned.1.call-start = ((), (), s32[]{:S(2)}) async-start(), calls=%async_computation.3 | async-start | bytes 1310720 | tf_op jit(solution)/shard_map/while/body/eval_jaxpr/reduce_scatter | solution.py:58
  487.4 45.5 %reduce-scatter.3.cloned.1.call-start = ((), (), s32[]{:S(2)}) async-start(), calls=%async_computation.2 | async-start | bytes 2752512 | tf_op jit(solution)/shard_map/while/body/eval_jaxpr/reduce_scatter | solution.py:40
  487.4 9.4 %collective-permute-start = (f32[128,512]{1,0:T(8,128)}, f32[128,512]{1,0:T(8,128)S(1)}, u32[]{:S(2)}, u32[]{:S(2)}) collective-permute-start(f32[128,512]{1,0:T(8,128)} %get-tuple-element.343), channel_id=1, source_target_pairs={{0,24},{8,0},{16,8},{24,16},{1,25},{9,1},{17,9},{25,17},{2,26},{10... | collective-permute-start | bytes 786440 | tf_op jit(solution)/shard_map/while/body/eval_jaxpr/ppermute | solution.py:12
  524.3 65.0 %reduce-scatter.5.cloned.1.call-start = ((), (), s32[]{:S(2)}) async-start(), calls=%async_computation.3 | async-start | bytes 1310720 | tf_op jit(solution)/shard_map/while/body/eval_jaxpr/reduce_scatter | solution.py:58
  605.9 45.5 %reduce-scatter.3.cloned.1.call-start = ((), (), s32[]{:S(2)}) async-start(), calls=%async_computation.2 | async-start | bytes 2752512 | tf_op jit(solution)/shard_map/while/body/eval_jaxpr/reduce_scatter | solution.py:40
  605.9 9.4 %collective-permute-start = (f32[128,512]{1,0:T(8,128)}, f32[128,512]{1,0:T(8,128)S(1)}, u32[]{:S(2)}, u32[]{:S(2)}) collective-permute-start(f32[128,512]{1,0:T(8,128)} %get-tuple-element.343), channel_id=1, source_target_pairs={{0,24},{8,0},{16,8},{24,16},{1,25},{9,1},{17,9},{25,17},{2,26},{10... | collective-permute-start | bytes 786440 | tf_op jit(solution)/shard_map/while/body/eval_jaxpr/ppermute | solution.py:12
  642.8 65.0 %reduce-scatter.5.cloned.1.call-start = ((), (), s32[]{:S(2)}) async-start(), calls=%async_computation.3 | async-start | bytes 1310720 | tf_op jit(solution)/shard_map/while/body/eval_jaxpr/reduce_scatter | solution.py:58
  724.4 45.5 %reduce-scatter.3.cloned.1.call-start = ((), (), s32[]{:S(2)}) async-start(), calls=%async_computation.2 | async-start | bytes 2752512 | tf_op jit(solution)/shard_map/while/body/eval_jaxpr/reduce_scatter | solution.py:40
  724.4 9.4 %collective-permute-start = (f32[128,512]{1,0:T(8,128)}, f32[128,512]{1,0:T(8,128)S(1)}, u32[]{:S(2)}, u32[]{:S(2)}) collective-permute-start(f32[128,512]{1,0:T(8,128)} %get-tuple-element.343), channel_id=1, source_target_pairs={{0,24},{8,0},{16,8},{24,16},{1,25},{9,1},{17,9},{25,17},{2,26},{10... | collective-permute-start | bytes 786440 | tf_op jit(solution)/shard_map/while/body/eval_jaxpr/ppermute | solution.py:12
  761.3 65.0 %reduce-scatter.5.cloned.1.call-start = ((), (), s32[]{:S(2)}) async-start(), calls=%async_computation.3 | async-start | bytes 1310720 | tf_op jit(solution)/shard_map/while/body/eval_jaxpr/reduce_scatter | solution.py:58
  842.9 9.4 %collective-permute-start.1 = (f32[128,512]{1,0:T(8,128)}, f32[128,512]{1,0:T(8,128)S(1)}, u32[]{:S(2)}, u32[]{:S(2)}) collective-permute-start(f32[128,512]{1,0:T(8,128)} %get-tuple-element.223), channel_id=1, source_target_pairs={{0,24},{8,0},{16,8},{24,16},{1,25},{9,1},{17,9},{25,17},{2,26},{10... | collective-permute-start | bytes 786440 | tf_op jit(solution)/shard_map/ppermute | solution.py:12
  (7 other events, 258.8 us)
Sparse Core Ops, SparseCore 0:
  46.7 11.8 reduce-scatter.2
  86.5 28.5 reduce-scatter.4
  168.7 8.5 reduce-scatter.2
  205.1 28.5 reduce-scatter.4
  287.3 8.4 reduce-scatter.2
  323.6 28.5 reduce-scatter.4
  405.9 8.4 reduce-scatter.2
  442.2 28.5 reduce-scatter.4
  524.4 8.4 reduce-scatter.2
  560.7 28.5 reduce-scatter.4
  642.9 8.4 reduce-scatter.2
  679.2 28.5 reduce-scatter.4
  761.5 8.4 reduce-scatter.2
  797.7 28.5 reduce-scatter.4
where the time goes:
time: 882 us; the launch traced here: 881 us
  waiting for transfers between devices  319 us (36%)
  blocking collectives  256 us (29%)
  matrix products  228 us (26%)
  other arithmetic  39.4 us (4%)
  starting transfers between devices  21 us (2%)
  between operations  13.7 us (2%)
    reduce_scatter x7, waiting for transfers between devices, layer_step(): lax.psum_scatter(first + second, 'col', scatter_dimension=0, tiled=True)  201 us
    all_gather x7, blocking collectives, layer_step(): wide = lax.all_gather(gy, 'col', axis=1, tiled=True)  112 us
    psum x7, blocking collectives, layer_step(): inner = lax.psum(jnp.sum(scaled * xf, axis=1), ('row', 'col'))[:, None] / D  95.9 us
    dot_general x7, matrix products, layer_step(): lax.dot_general(wide, wd, (((1,), (1,)), ((), ())), preferred_element_typ...  79.4 us
    dot_general x7, matrix products, layer_step(): lax.dot_general(wu, grad_up, (((1,), (1,)), ((), ())), preferred_element_...  76.5 us
    dot_general x7, matrix products, layer_step(): lax.dot_general(wg, grad_gate, (((1,), (1,)), ((), ())), preferred_elemen...  69.4 us
    reduce_scatter x7, waiting for transfers between devices, layer_step(): ga = lax.psum_scatter(ga_part, 'row', scatter_dimension=1, tiled=True)  63.1 us
    ppermute x8, waiting for transfers between devices, shifted(): lax.ppermute(x, axis, [(i, (i + by) % devices) for i in range(devices)])  54.8 us
  transfers between devices with their start and end apart: 22, of which 22 were waited for; matrix products, arithmetic and copies ran while one was open for 0% of the time, Pallas kernels for 0%

commit v1 on v0

--- a/solution.py
+++ b/solution.py
@@ -58,7 +58,10 @@
         normgrad = lax.psum_scatter(first + second, "col", scatter_dimension=0, tiled=True).T
         rstd = lax.rsqrt(sumsq / D + eps)[:, None]
         scaled = gain * normgrad
-        inner = lax.psum(jnp.sum(scaled * xf, axis=1), ("row", "col"))[:, None] / D
+        inner = (
+            jnp.sum(lax.all_gather(jnp.sum(scaled * xf, axis=1), ("row", "col")), axis=0)[:, None]
+            / D
+        )
         updated = carry + rstd * scaled - xf * (rstd * rstd * rstd) * inner
         active = jnp.logical_and(step >= micro, step - micro < sections)
         return jnp.where(active, updated, carry)

time: 882 us -> 980 us (1.11)
  blocking collectives: 256 us -> 359 us
    all_gather x0 -> x7, blocking collectives: none -> 89.5 us  [layer_step(): lax.all_gather(jnp.sum(scaled * xf, axis=1), ('row', 'col'))]
    psum x7, blocking collectives: 95.9 us -> 112 us  [layer_step(): sumsq = lax.psum(jnp.sum(xf * xf, axis=1), ('row', 'col'))]
where the time goes in v1:
time: 980 us; the launch traced here: 978 us
  blocking collectives  359 us (37%)
  waiting for transfers between devices  314 us (32%)
  matrix products  228 us (23%)
  other arithmetic  39.7 us (4%)
  starting transfers between devices  21 us (2%)
  between operations  13.7 us (1%)
    reduce_scatter x7, waiting for transfers between devices, layer_step(): lax.psum_scatter(first + second, 'col', scatter_dimension=0, tiled=True)  201 us
    psum x7, blocking collectives, layer_step(): sumsq = lax.psum(jnp.sum(xf * xf, axis=1), ('row', 'col'))  112 us
    all_gather x7, blocking collectives, layer_step(): wide = lax.all_gather(gy, 'col', axis=1, tiled=True)  110 us
    all_gather x7, blocking collectives, layer_step(): lax.all_gather(jnp.sum(scaled * xf, axis=1), ('row', 'col'))  89.5 us
    dot_general x7, matrix products, layer_step(): lax.dot_general(wide, wd, (((1,), (1,)), ((), ())), preferred_element_typ...  79.4 us
    dot_general x7, matrix products, layer_step(): lax.dot_general(wu, grad_up, (((1,), (1,)), ((), ())), preferred_element_...  76.5 us
    dot_general x7, matrix products, layer_step(): lax.dot_general(wg, grad_gate, (((1,), (1,)), ((), ())), preferred_elemen...  69.4 us
    reduce_scatter x7, waiting for transfers between devices, layer_step(): ga = lax.psum_scatter(ga_part, 'row', scatter_dimension=1, tiled=True)  63.6 us
  transfers between devices with their start and end apart: 22, of which 22 were waited for; matrix products, arithmetic and copies ran while one was open for 0% of the time, Pallas kernels for 0%

profile of v1, /device:TPU:0, one launch (start us, length us, event | category | flops | bytes accessed | tf_op | source)
XLA Modules:
  0.0 978.1 jit_solution(1088504964399017799)
XLA Ops:
  10.2 931.3 %while.15 = (s32[]{:T(128)}, f32[128,512]{1,0:T(8,128)}, s32[]{:T(128)}, f32[4,128,512]{2,1,0:T(8,128)S(1)}, f32[1,512]{1,0:T(1,128)}, /*index=5*/bf16[3584,2048...) while((s32[]{:T(128)}, f32[128,512]{1,0:T(8,128)}, ...), condition=%wide.region_7.8_spmd, body=%wide.region_0.7_spmd.sunk | while | flops 5641700864 | bytes 72773232 | solution.py:69
  20.1 15.1 %all_gather.53 = bf16[128,2048]{1,0:T(8,128)(2,1)S(1)} all-gather(bf16[128,512]{1,0:T(8,128)(2,1)S(1)} %convert_element_type.72), channel_id=1, replica_groups=mesh['section'=4,'row'=2,'col'=4] {'col'}, dimensions={1}, use_global_device_ids=true | all-gather | bytes 655360 | tf_op jit(solution)/shard_map/while/body/eval_jaxpr/all_gather | solution.py:36
  86.4 28.7 %reduce-scatter.5.cloned.1.call-done = f32[512,128]{0,1:T(8,128)} async-done(((f32[2048,128]{0,1:T(8,128)}), f32[512,128]{0,1:T(8,128)}) %reduce-scatter.5.cloned.1.call-update) | async-done | bytes 262160 | tf_op jit(solution)/shard_map/while/body/eval_jaxpr/reduce_scatter | solution.py:58
  116.2 12.8 %all-gather.3 = f32[8,1,128]{2,1,0:T(1,128)S(1)} all-gather(f32[1,1,128]{2,1,0:T(1,128)S(1)} %bitcast.111), channel_id=2, replica_groups=mesh['section'=4,'row'=2,'col'=4] {'row','col'}, dimensions={0}, use_global_device_ids=true | all-gather | bytes 4608 | tf_op jit(solution)/shard_map/while/body/eval_jaxpr/all_gather | solution.py:62
  129.0 15.9 %psum.23 = f32[128]{0:T(128)S(1)} all-reduce(f32[128]{0:T(128)S(1)} %get-tuple-element.312), channel_id=1, replica_groups=mesh['section'=4,'row'=2,'col'=4] {'row','col'}, use_global_device_ids=true, to_apply=%region_2.2 | all-reduce | flops 128 | bytes 1024 | tf_op jit(solution)/shard_map/while/body/eval_jaxpr/psum | solution.py:34
  155.3 15.8 %all_gather.53 = bf16[128,2048]{1,0:T(8,128)(2,1)S(1)} all-gather(bf16[128,512]{1,0:T(8,128)(2,1)S(1)} %convert_element_type.72), channel_id=1, replica_groups=mesh['section'=4,'row'=2,'col'=4] {'col'}, dimensions={1}, use_global_device_ids=true | all-gather | bytes 655360 | tf_op jit(solution)/shard_map/while/body/eval_jaxpr/all_gather | solution.py:36
  218.9 28.7 %reduce-scatter.5.cloned.1.call-done = f32[512,128]{0,1:T(8,128)} async-done(((f32[2048,128]{0,1:T(8,128)}), f32[512,128]{0,1:T(8,128)}) %reduce-scatter.5.cloned.1.call-update) | async-done | bytes 262160 | tf_op jit(solution)/shard_map/while/body/eval_jaxpr/reduce_scatter | solution.py:58
  261.5 15.9 %psum.23 = f32[128]{0:T(128)S(1)} all-reduce(f32[128]{0:T(128)S(1)} %get-tuple-element.312), channel_id=1, replica_groups=mesh['section'=4,'row'=2,'col'=4] {'row','col'}, use_global_device_ids=true, to_apply=%region_2.2 | all-reduce | flops 128 | bytes 1024 | tf_op jit(solution)/shard_map/while/body/eval_jaxpr/psum | solution.py:34
  287.8 15.8 %all_gather.53 = bf16[128,2048]{1,0:T(8,128)(2,1)S(1)} all-gather(bf16[128,512]{1,0:T(8,128)(2,1)S(1)} %convert_element_type.72), channel_id=1, replica_groups=mesh['section'=4,'row'=2,'col'=4] {'col'}, dimensions={1}, use_global_device_ids=true | all-gather | bytes 655360 | tf_op jit(solution)/shard_map/while/body/eval_jaxpr/all_gather | solution.py:36
  351.3 28.7 %reduce-scatter.5.cloned.1.call-done = f32[512,128]{0,1:T(8,128)} async-done(((f32[2048,128]{0,1:T(8,128)}), f32[512,128]{0,1:T(8,128)}) %reduce-scatter.5.cloned.1.call-update) | async-done | bytes 262160 | tf_op jit(solution)/shard_map/while/body/eval_jaxpr/reduce_scatter | solution.py:58
  393.9 15.9 %psum.23 = f32[128]{0:T(128)S(1)} all-reduce(f32[128]{0:T(128)S(1)} %get-tuple-element.312), channel_id=1, replica_groups=mesh['section'=4,'row'=2,'col'=4] {'row','col'}, use_global_device_ids=true, to_apply=%region_2.2 | all-reduce | flops 128 | bytes 1024 | tf_op jit(solution)/shard_map/while/body/eval_jaxpr/psum | solution.py:34
  420.2 15.8 %all_gather.53 = bf16[128,2048]{1,0:T(8,128)(2,1)S(1)} all-gather(bf16[128,512]{1,0:T(8,128)(2,1)S(1)} %convert_element_type.72), channel_id=1, replica_groups=mesh['section'=4,'row'=2,'col'=4] {'col'}, dimensions={1}, use_global_device_ids=true | all-gather | bytes 655360 | tf_op jit(solution)/shard_map/while/body/eval_jaxpr/all_gather | solution.py:36
  483.8 28.7 %reduce-scatter.5.cloned.1.call-done = f32[512,128]{0,1:T(8,128)} async-done(((f32[2048,128]{0,1:T(8,128)}), f32[512,128]{0,1:T(8,128)}) %reduce-scatter.5.cloned.1.call-update) | async-done | bytes 262160 | tf_op jit(solution)/shard_map/while/body/eval_jaxpr/reduce_scatter | solution.py:58
  526.4 15.9 %psum.23 = f32[128]{0:T(128)S(1)} all-reduce(f32[128]{0:T(128)S(1)} %get-tuple-element.312), channel_id=1, replica_groups=mesh['section'=4,'row'=2,'col'=4] {'row','col'}, use_global_device_ids=true, to_apply=%region_2.2 | all-reduce | flops 128 | bytes 1024 | tf_op jit(solution)/shard_map/while/body/eval_jaxpr/psum | solution.py:34
  552.7 15.8 %all_gather.53 = bf16[128,2048]{1,0:T(8,128)(2,1)S(1)} all-gather(bf16[128,512]{1,0:T(8,128)(2,1)S(1)} %convert_element_type.72), channel_id=1, replica_groups=mesh['section'=4,'row'=2,'col'=4] {'col'}, dimensions={1}, use_global_device_ids=true | all-gather | bytes 655360 | tf_op jit(solution)/shard_map/while/body/eval_jaxpr/all_gather | solution.py:36
  616.2 28.7 %reduce-scatter.5.cloned.1.call-done = f32[512,128]{0,1:T(8,128)} async-done(((f32[2048,128]{0,1:T(8,128)}), f32[512,128]{0,1:T(8,128)}) %reduce-scatter.5.cloned.1.call-update) | async-done | bytes 262160 | tf_op jit(solution)/shard_map/while/body/eval_jaxpr/reduce_scatter | solution.py:58
  658.8 15.9 %psum.23 = f32[128]{0:T(128)S(1)} all-reduce(f32[128]{0:T(128)S(1)} %get-tuple-element.312), channel_id=1, replica_groups=mesh['section'=4,'row'=2,'col'=4] {'row','col'}, use_global_device_ids=true, to_apply=%region_2.2 | all-reduce | flops 128 | bytes 1024 | tf_op jit(solution)/shard_map/while/body/eval_jaxpr/psum | solution.py:34
  685.1 15.8 %all_gather.53 = bf16[128,2048]{1,0:T(8,128)(2,1)S(1)} all-gather(bf16[128,512]{1,0:T(8,128)(2,1)S(1)} %convert_element_type.72), channel_id=1, replica_groups=mesh['section'=4,'row'=2,'col'=4] {'col'}, dimensions={1}, use_global_device_ids=true | all-gather | bytes 655360 | tf_op jit(solution)/shard_map/while/body/eval_jaxpr/all_gather | solution.py:36
  748.7 28.7 %reduce-scatter.5.cloned.1.call-done = f32[512,128]{0,1:T(8,128)} async-done(((f32[2048,128]{0,1:T(8,128)}), f32[512,128]{0,1:T(8,128)}) %reduce-scatter.5.cloned.1.call-update) | async-done | bytes 262160 | tf_op jit(solution)/shard_map/while/body/eval_jaxpr/reduce_scatter | solution.py:58
  791.3 15.9 %psum.23 = f32[128]{0:T(128)S(1)} all-reduce(f32[128]{0:T(128)S(1)} %get-tuple-element.312), channel_id=1, replica_groups=mesh['section'=4,'row'=2,'col'=4] {'row','col'}, use_global_device_ids=true, to_apply=%region_2.2 | all-reduce | flops 128 | bytes 1024 | tf_op jit(solution)/shard_map/while/body/eval_jaxpr/psum | solution.py:34
  817.6 15.8 %all_gather.53 = bf16[128,2048]{1,0:T(8,128)(2,1)S(1)} all-gather(bf16[128,512]{1,0:T(8,128)(2,1)S(1)} %convert_element_type.72), channel_id=1, replica_groups=mesh['section'=4,'row'=2,'col'=4] {'col'}, dimensions={1}, use_global_device_ids=true | all-gather | bytes 655360 | tf_op jit(solution)/shard_map/while/body/eval_jaxpr/all_gather | solution.py:36
  881.1 28.7 %reduce-scatter.5.cloned.1.call-done = f32[512,128]{0,1:T(8,128)} async-done(((f32[2048,128]{0,1:T(8,128)}), f32[512,128]{0,1:T(8,128)}) %reduce-scatter.5.cloned.1.call-update) | async-done | bytes 262160 | tf_op jit(solution)/shard_map/while/body/eval_jaxpr/reduce_scatter | solution.py:58
  923.7 15.9 %psum.23 = f32[128]{0:T(128)S(1)} all-reduce(f32[128]{0:T(128)S(1)} %get-tuple-element.312), channel_id=1, replica_groups=mesh['section'=4,'row'=2,'col'=4] {'row','col'}, use_global_device_ids=true, to_apply=%region_2.2 | all-reduce | flops 128 | bytes 1024 | tf_op jit(solution)/shard_map/while/body/eval_jaxpr/psum | solution.py:34
  953.1 13.9 %psum.21 = f32[8]{0:T(128)S(1)} all-reduce(f32[8]{0:T(128)S(1)} %fusion.16), channel_id=1, replica_groups=mesh['section'=4,'row'=2,'col'=4] {'row','col'}, use_global_device_ids=true, to_apply=%region_8.9 | all-reduce | flops 8 | bytes 64 | tf_op jit(solution)/shard_map/psum | solution.py:73
  (165 shorter events, 514.6 us)
Async XLA Ops:
  7.2 959.8 %copy-start = (f32[1,8,128,512]{3,2,1,0:T(8,128)S(1)}, f32[1,8,128,512]{3,2,1,0:T(8,128)}, u32[]{:S(2)}) copy-start(f32[1,8,128,512]{3,2,1,0:T(8,128)} %param.14) | copy-start | bytes 6291460
  10.2 48.5 %reduce-scatter.3.cloned.1.call-start = ((), (), s32[]{:S(2)}) async-start(), calls=%async_computation.2 | async-start | bytes 2752512 | tf_op jit(solution)/shard_map/while/body/eval_jaxpr/reduce_scatter | solution.py:40
  10.2 9.9 %collective-permute-start = (f32[128,512]{1,0:T(8,128)}, f32[128,512]{1,0:T(8,128)S(1)}, u32[]{:S(2)}, u32[]{:S(2)}) collective-permute-start(f32[128,512]{1,0:T(8,128)} %get-tuple-element.335), channel_id=1, source_target_pairs={{0,24},{8,0},{16,8},{24,16},{1,25},{9,1},{17,9},{25,17},{2,26},{10... | collective-permute-start | bytes 786440 | tf_op jit(solution)/shard_map/while/body/eval_jaxpr/ppermute | solution.py:12
  46.6 68.5 %reduce-scatter.5.cloned.1.call-start = ((), (), s32[]{:S(2)}) async-start(), calls=%async_computation.3 | async-start | bytes 1310720 | tf_op jit(solution)/shard_map/while/body/eval_jaxpr/reduce_scatter | solution.py:58
  75.4 39.7 %copy-start.2 = (f32[1,512]{1,0:T(1,128)S(1)}, f32[1,512]{1,0:T(1,128)}, u32[]{:S(2)}) copy-start(f32[1,512]{1,0:T(1,128)} %get-tuple-element.357) | copy-start | bytes 6148 | tf_op jit(solution)/shard_map/while
  146.8 44.4 %reduce-scatter.3.cloned.1.call-start = ((), (), s32[]{:S(2)}) async-start(), calls=%async_computation.2 | async-start | bytes 2752512 | tf_op jit(solution)/shard_map/while/body/eval_jaxpr/reduce_scatter | solution.py:40
  146.8 8.6 collective-permute-start
  182.5 65.1 %reduce-scatter.5.cloned.1.call-start = ((), (), s32[]{:S(2)}) async-start(), calls=%async_computation.3 | async-start | bytes 1310720 | tf_op jit(solution)/shard_map/while/body/eval_jaxpr/reduce_scatter | solution.py:58
  279.2 44.4 %reduce-scatter.3.cloned.1.call-start = ((), (), s32[]{:S(2)}) async-start(), calls=%async_computation.2 | async-start | bytes 2752512 | tf_op jit(solution)/shard_map/while/body/eval_jaxpr/reduce_scatter | solution.py:40
  279.2 8.5 collective-permute-start
  314.9 65.1 %reduce-scatter.5.cloned.1.call-start = ((), (), s32[]{:S(2)}) async-start(), calls=%async_computation.3 | async-start | bytes 1310720 | tf_op jit(solution)/shard_map/while/body/eval_jaxpr/reduce_scatter | solution.py:58
  411.7 44.4 %reduce-scatter.3.cloned.1.call-start = ((), (), s32[]{:S(2)}) async-start(), calls=%async_computation.2 | async-start | bytes 2752512 | tf_op jit(solution)/shard_map/while/body/eval_jaxpr/reduce_scatter | solution.py:40
  411.7 8.5 collective-permute-start
  447.4 65.1 %reduce-scatter.5.cloned.1.call-start = ((), (), s32[]{:S(2)}) async-start(), calls=%async_computation.3 | async-start | bytes 1310720 | tf_op jit(solution)/shard_map/while/body/eval_jaxpr/reduce_scatter | solution.py:58
  544.1 44.4 %reduce-scatter.3.cloned.1.call-start = ((), (), s32[]{:S(2)}) async-start(), calls=%async_computation.2 | async-start | bytes 2752512 | tf_op jit(solution)/shard_map/while/body/eval_jaxpr/reduce_scatter | solution.py:40
  544.1 8.5 collective-permute-start
  579.8 65.1 %reduce-scatter.5.cloned.1.call-start = ((), (), s32[]{:S(2)}) async-start(), calls=%async_computation.3 | async-start | bytes 1310720 | tf_op jit(solution)/shard_map/while/body/eval_jaxpr/reduce_scatter | solution.py:58
  676.6 44.4 %reduce-scatter.3.cloned.1.call-start = ((), (), s32[]{:S(2)}) async-start(), calls=%async_computation.2 | async-start | bytes 2752512 | tf_op jit(solution)/shard_map/while/body/eval_jaxpr/reduce_scatter | solution.py:40
  676.6 8.5 collective-permute-start
  712.3 65.1 %reduce-scatter.5.cloned.1.call-start = ((), (), s32[]{:S(2)}) async-start(), calls=%async_computation.3 | async-start | bytes 1310720 | tf_op jit(solution)/shard_map/while/body/eval_jaxpr/reduce_scatter | solution.py:58
  809.0 44.4 %reduce-scatter.3.cloned.1.call-start = ((), (), s32[]{:S(2)}) async-start(), calls=%async_computation.2 | async-start | bytes 2752512 | tf_op jit(solution)/shard_map/while/body/eval_jaxpr/reduce_scatter | solution.py:40
  809.0 8.5 collective-permute-start
  844.7 65.1 %reduce-scatter.5.cloned.1.call-start = ((), (), s32[]{:S(2)}) async-start(), calls=%async_computation.3 | async-start | bytes 1310720 | tf_op jit(solution)/shard_map/while/body/eval_jaxpr/reduce_scatter | solution.py:58
  941.5 8.5 collective-permute-start.1
  (7 other events, 258.6 us)
Sparse Core Ops, SparseCore 0:
  46.7 11.8 reduce-scatter.2
  86.5 28.5 reduce-scatter.4
  182.6 8.5 reduce-scatter.2
  219.0 28.5 reduce-scatter.4
  315.1 8.5 reduce-scatter.2
  351.4 28.5 reduce-scatter.4
  447.5 8.5 reduce-scatter.2
  483.9 28.5 reduce-scatter.4
  580.0 8.5 reduce-scatter.2
  616.3 28.5 reduce-scatter.4
  712.4 8.5 reduce-scatter.2
  748.8 28.5 reduce-scatter.4
  844.8 8.5 reduce-scatter.2
  881.2 28.5 reduce-scatter.4
